TPU v7x, 512 devices: a whole 4x4x16 slice. The times are simulated.
512 devices in a mesh: rows: 64 (over y, z), cols: 8 (over x, core).
Axes of the slice: x: 4, y: 4, z: 16, core: 2. Of those that a mesh axis runs over, the one named last changes fastest.
Arguments:
- images: float32 [512, 32, 128], P('rows'), may hold values from -6 to 6
- gauge_pixel: int32 [131072], P('rows'), may hold values from 0 to 32767
- row_mask: int32 [131072], P('rows'), may hold values 0 or 1
- gauge_counts: int32 [64], P('rows'), may hold values from 1 to 2048, as said below
- targets: float32 [131072], P('rows'), may hold values from -10 to 10
- theta: float32 [64, 8], replicated, may hold values from -2.5 to 2.5
- amplitude: float32 [64], replicated, may hold values from 0.5 to 1.5
- damping: float32 [], replicated, may hold values from 0.05 to 0.3
Outputs:
- r_factor: float32 [512, 512], replicated
- new_theta: float32 [64, 8], replicated
- predicted: float32 [131072], P(('rows', 'cols'))
Inputs may be any that keep to these rules, and one draw needn't show every extreme that they name: The slots in use on an index of rows are its first gauge_counts slots; one index of rows uses all 2048.
All inputs are finite; a program needn't handle non-finite values. No bound on the sum of `row_mask` on one device may be relied on, other than what follows from the above.
Results may differ from a plain program's by a relative error of at most 0.0003.
Values sent between devices are 32-bit elements; how exact they have to be, the bound alone decides.
A program may use at most 64 MiB of HBM per device.

v0:
```python
import jax
import jax.numpy as jnp
from jax import lax
from jax.sharding import PartitionSpec as P

BLOCK = 256
y_orders = [0, 1, 0, 2, 1, 0, 0, 0]
x_orders = [0, 0, 1, 0, 1, 2, 0, 2]
sigmas = [1.5, 1.5, 1.5, 1.5, 1.5, 1.5, 3.0, 3.0]


def kernel_values(spacing, deriv_order, width_sigma):
    envelope = jnp.exp(-spacing * spacing / (2.0 * width_sigma * width_sigma))
    if deriv_order == 1:
        return -spacing / width_sigma**2 * envelope
    if deriv_order == 2:
        return (spacing * spacing / width_sigma**4 - 1.0 / width_sigma**2) * envelope
    return envelope


def kernel_table(length, deriv_order, width_sigma):
    places = jnp.arange(length)
    spacing = (places[:, None] - places[None, :]).astype(jnp.float32)
    sample = jnp.arange(-12, 13).astype(jnp.float32)
    scaling = jnp.sqrt(jnp.sum(kernel_values(sample, deriv_order, width_sigma) ** 2))
    return kernel_values(spacing, deriv_order, width_sigma) / scaling


def features(clip_tiles):
    height = clip_tiles.shape[1]
    breadth = clip_tiles.shape[2]
    left_tabs = jnp.stack(
        [kernel_table(height, y_orders[which], sigmas[which]) for which in range(8)]
    )
    right_tabs = jnp.stack(
        [kernel_table(breadth, x_orders[which], sigmas[which]) for which in range(8)]
    )
    partial_conv = jnp.einsum(
        "kij,cjw->kciw", left_tabs, clip_tiles, precision=lax.Precision.HIGHEST
    )
    full_conv = jnp.einsum(
        "kciw,kvw->kciv", partial_conv, right_tabs, precision=lax.Precision.HIGHEST
    )
    return full_conv.reshape(full_conv.shape[0], -1)


def outer_rows(slope, phi):
    return (slope[:, :, None] * phi[:, None, :]).reshape(slope.shape[0], -1)


def solve_step(lower, rhs):
    inner = lax.linalg.triangular_solve(lower, rhs[:, None], left_side=True, lower=True)
    outer = lax.linalg.triangular_solve(lower, inner, left_side=True, lower=True, transpose_a=True)
    return -outer[:, 0]


def on_device(images, gauge_pixel, row_mask, gauge_counts, targets, theta, amplitude, damping):
    ncols = lax.axis_size("cols")
    column = lax.axis_index("cols")
    slots = gauge_pixel.shape[0]
    share = slots // ncols
    channels = theta.shape[0]
    basis_count = theta.shape[1]
    params = channels * basis_count
    local_width = channels // ncols
    own_params = local_width * basis_count
    count = gauge_counts[0]
    live = ((jnp.arange(slots) < count) & (row_mask == 1)).astype(jnp.float32)
    flat_feats = features(images)
    phi = jnp.take(flat_feats, gauge_pixel, axis=1).T
    act = jnp.tanh(jnp.dot(phi, theta.T, precision=lax.Precision.HIGHEST))
    model = jnp.dot(act, amplitude, precision=lax.Precision.HIGHEST)
    resid = live * (model - targets)
    slope = live[:, None] * amplitude[None, :] * (1.0 - act * act)

    def block_rows(values):
        return lax.dynamic_slice_in_dim(values, column * share, share, 0)

    def pick(values):
        return block_rows(values)

    local_slope = lax.dynamic_slice_in_dim(slope, column * local_width, local_width, 1)
    jac_cols = outer_rows(local_slope, phi)
    prefix = jnp.clip(count - column * share, 0, share)
    assigned = lax.all_to_all(jac_cols, "cols", split_axis=0, concat_axis=1, tiled=True)
    assigned_resid = pick(resid)
    trips = (prefix + BLOCK - 1) // BLOCK

    def add_block(which, carry):
        gram = carry[0] + lax.dot_general(
            assigned,
            assigned,
            (((0,), (0,)), ((), ())),
            precision=lax.Precision.HIGHEST,
            preferred_element_type=jnp.float32,
        )
        grad = carry[1] + jnp.dot(assigned_resid, assigned, precision=lax.Precision.HIGHEST)
        return (gram, grad)

    start = (jnp.zeros((params, params), jnp.float32), jnp.zeros((params,), jnp.float32))
    gram_part, grad_part = lax.fori_loop(0, trips, add_block, start)
    live_part = jnp.sum(pick(live))
    gram, grad, total = lax.psum((gram_part, grad_part, live_part), ("rows", "cols"))
    normal = gram / total + damping * jnp.eye(params, dtype=jnp.float32)
    lower = jnp.linalg.cholesky(normal)
    step = solve_step(lower, grad / total)
    local_step = lax.dynamic_slice_in_dim(step, column * own_params, own_params, 0)
    linear_part = lax.psum_scatter(
        jnp.dot(jac_cols, local_step, precision=lax.Precision.HIGHEST),
        "cols",
        scatter_dimension=0,
        tiled=True,
    )
    predicted = block_rows(resid) + linear_part
    return (lower.T, theta + step.reshape(channels, basis_count), predicted)


def solution(mesh):
    return jax.shard_map(
        on_device,
        mesh=mesh,
        in_specs=(P("rows", None, None), P("rows"), P("rows"), P("rows"), P("rows"), P(), P(), P()),
        out_specs=(P(), P(), P(("rows", "cols"))),
        check_vma=False,
    )
```

profile of v0, /device:TPU:8, one launch (start us, length us, event | category | flops | bytes accessed | tf_op | source)
XLA Modules:
  0.0 705.4 jit_solution(6471413244750945603)
XLA Ops:
  16.3 1.0 convolution_bitcast_fusion
  17.3 1.1 fusion.15
  18.4 8.6 %copy.61 = f32[8,8,32,128]{0,3,2,1:T(8,128)} copy(f32[8,8,32,128]{3,2,1,0:T(8,128)S(1)} %fusion.15) | data formatting | bytes 2097152 | tf_op jit(solution)/shard_map/reshape | solution.py:44
  27.0 11.2 %gather_fusion = f32[2048,8]{1,0:T(8,128)S(1)} fusion(f32[8,32768]{0,1:T(8,128)} %bitcast.185, s32[2048]{0:T(1024)S(1)} %fusion.50), kind=kCustom, calls=%fused_computation | custom fusion | bytes 139264 | tf_op jit(solution)/shard_map/jit(_take)/gather | solution.py:70
  38.8 1.3 convolution_tanh_fusion
  40.6 1.0 copy.43
  41.5 4.3 all-to-all-start
  46.3 0.8 dynamic-slice_select_fusion
  47.1 9.1 %all-to-all-done = f32[8,256,64]{1,2,0:T(8,128)S(1)} async-done(((f32[8,256,64]{1,2,0:T(8,128)}), f32[8,256,64]{1,2,0:T(8,128)S(1)}, u32[]{:S(2)}, u32[]{:S(2)}) %all-to-all-start) | async-done | bytes 524320 | tf_op jit(solution)/shard_map/all_to_all | solution.py:85
  56.1 1.0 fusion.83
  58.2 1.3 copy.45
  60.9 1.3 dynamic-slice.4
  62.9 108.7 %all-reduce.2 = (f32[]{:T(128)}, f32[512]{0:T(512)S(1)}) all-reduce(f32[]{:T(128)} %dynamic-slice_reduce_fusion, f32[512]{0:T(512)S(1)} %get-tuple-element.82), channel_id=1, replica_groups=mesh['rows'=64,'cols'=8] {'rows','cols'}, use_global_device_ids=true, to_apply=%region_9.0 | all-reduce | flops 513 | bytes 4104 | tf_op jit(solution)/shard_map/psum | solution.py:103
  172.3 363.3 %all-reduce.5.cloned.1.call-done = f32[512,512]{0,1:T(8,128)} async-done(((f32[512,512]{0,1:T(8,128)}), f32[512,512]{0,1:T(8,128)}) %all-reduce.5.cloned.1.call-update) | async-done | bytes 1048592 | tf_op jit(solution)/shard_map/psum | solution.py:103
  535.6 2.0 select_add_fusion
  537.9 2.1 fusion.12
  540.1 11.7 %cholesky.103 = f32[128,128]{1,0:T(8,128)S(1)} custom-call(f32[128,128]{1,0:T(8,128)S(1)} %cholesky.263), custom_call_target="Cholesky" | custom-call | tf_op jit(solution)/shard_map/jit(cholesky)/cholesky | solution.py:105
  551.8 9.8 %custom-call.32 = f32[1,128,128]{1,2,0:T(8,128)S(1)} custom-call(f32[1,128,128]{2,1,0:T(8,128)S(1)} %get-tuple-element.162), custom_call_target="InvertDiagBlocksLowerTriangular" | custom-call | tf_op jit(solution)/shard_map/jit(cholesky)/cholesky | solution.py:105
  562.3 11.7 %cholesky.215 = f32[128,128]{1,0:T(8,128)S(1)} custom-call(f32[128,128]{1,0:T(8,128)S(1)} %cholesky.267), custom_call_target="Cholesky" | custom-call | tf_op jit(solution)/shard_map/jit(cholesky)/cholesky | solution.py:105
  574.5 9.9 %custom-call.33 = f32[1,128,128]{1,2,0:T(8,128)S(1)} custom-call(f32[1,128,128]{2,1,0:T(8,128)S(1)} %get-tuple-element.160), custom_call_target="InvertDiagBlocksLowerTriangular" | custom-call | tf_op jit(solution)/shard_map/jit(cholesky)/cholesky | solution.py:105
  585.5 11.7 %cholesky.236 = f32[128,128]{1,0:T(8,128)S(1)} custom-call(f32[128,128]{1,0:T(8,128)S(1)} %cholesky.272), custom_call_target="Cholesky" | custom-call | tf_op jit(solution)/shard_map/jit(cholesky)/cholesky | solution.py:105
  597.3 9.8 %custom-call.34 = f32[1,128,128]{1,2,0:T(8,128)S(1)} custom-call(f32[1,128,128]{2,1,0:T(8,128)S(1)} %get-tuple-element.158), custom_call_target="InvertDiagBlocksLowerTriangular" | custom-call | tf_op jit(solution)/shard_map/jit(cholesky)/cholesky | solution.py:105
  607.9 11.9 %cholesky.253 = f32[128,128]{1,0:T(8,128)S(1)} custom-call(f32[128,128]{1,0:T(8,128)S(1)} %convolution_subtract_fusion.2), custom_call_target="Cholesky" | custom-call | tf_op jit(solution)/shard_map/jit(cholesky)/cholesky | solution.py:105
  620.0 0.7 compare_reduce_fusion.1
  624.5 1.2 fusion.13
  625.8 11.3 %while.16 = (s32[]{:T(128)}, f32[512,512]{0,1:T(8,128)S(1)}, s32[4,2]{0,1:T(2,128)S(1)}, f32[4,128,128]{2,1,0:T(8,128)}, s32[]{:T(128)}) while((s32[]{:T(128)}, f32[512,512]{0,1:T(8,128)S(1)}, s32[4,2]{0,1:T(2,128)S(1)}, f32[4,128,128]{2,1,0:T(8,128)}, s32[]{:T(128)}) %tuple.61), condition=%wide.while_cond, body=%wide.while_body.sunk | while | flops 2 | bytes 393829 | solution.py:53
  626.4 1.4 dynamic-slice.12
  629.3 1.4 dynamic-slice.12
  632.1 1.4 dynamic-slice.12
  634.9 1.4 dynamic-slice.12
  637.1 40.1 %custom-call.35 = f32[4,128,128]{1,2,0:T(8,128)S(1)} custom-call(f32[4,128,128]{2,1,0:T(8,128)} %get-tuple-element.90), custom_call_target="InvertDiagBlocksLowerTriangular" | custom-call | tf_op jit(solution)/shard_map/triangular_solve | solution.py:53
  681.7 15.2 %all-reduce.1 = f32[2048]{0:T(1024)S(1)} all-reduce(f32[2048]{0:T(1024)S(1)} %bitcast.197), channel_id=2, replica_groups=mesh['rows'=64,'cols'=8] {'cols'}, use_global_device_ids=true, to_apply=%region_19.20.clone | all-reduce | flops 2048 | bytes 16384
  (116 shorter events, 25.3 us)
Async XLA Ops:
  7.2 9.1 %copy-start = (f32[8,32,128]{2,1,0:T(8,128)S(1)}, f32[8,32,128]{2,1,0:T(8,128)}, u32[]{:S(2)}) copy-start(f32[8,32,128]{2,1,0:T(8,128)} %param.10) | copy-start | bytes 393220
  7.2 31.7 %copy-start.1 = (f32[64,8]{0,1:T(8,128)S(1)}, f32[64,8]{0,1:T(8,128)}, u32[]{:S(2)}) copy-start(f32[64,8]{0,1:T(8,128)} %param.15) | copy-start | bytes 6148
  7.2 33.0 %copy-start.3 = (f32[64]{0:T(128)S(1)}, f32[64]{0:T(128)}, u32[]{:S(2)}) copy-start(f32[64]{0:T(128)} %param.16) | copy-start | bytes 772
  7.2 33.1 %copy-start.2 = (s32[2048]{0:T(1024)S(1)}, s32[2048]{0:T(1024)}, u32[]{:S(2)}) copy-start(s32[2048]{0:T(1024)} %param.12) | copy-start | bytes 24580
  41.5 14.6 %all-to-all-start = ((f32[8,256,64]{1,2,0:T(8,128)}), f32[8,256,64]{1,2,0:T(8,128)S(1)}, u32[]{:S(2)}, u32[]{:S(2)}) async-start(f32[8,256,64]{1,2,0:T(8,128)} %copy.43), calls=%async_computation | async-start | bytes 1048576 | tf_op jit(solution)/shard_map/all_to_all | solution.py:85
  45.8 489.8 %all-reduce.5.cloned.1.call-start = ((), (), s32[]{:S(2)}) async-start(), calls=%async_computation.1 | async-start | bytes 2097152 | tf_op jit(solution)/shard_map/psum | solution.py:103
Sparse Core Ops, SparseCore 0:
  59.6 475.9 all-reduce.4
where the time goes:
time: 712 us; the launch traced here: 705 us
  waiting for transfers between devices  372 us (52%)
  other arithmetic  133 us (19%)
  blocking collectives  124 us (17%)
  local copies, waits for them, and re-layouts  37.7 us (5%)
  between operations  22.7 us (3%)
  matrix products  10.9 us (2%)
    psum x1, waiting for transfers between devices, on_device(): lax.psum((gram_part, grad_part, live_part), ('rows', 'cols'))  363 us
    psum x1, blocking collectives, on_device(): lax.psum((gram_part, grad_part, live_part), ('rows', 'cols'))  109 us
    another operation x14, other arithmetic, on_device(): lower = jnp.linalg.cholesky(normal)  78.7 us
    another operation x3, other arithmetic, solve_step(): lax.linalg.triangular_solve(lower, inner, left_side=True, lower=True, tra...  41.4 us
    unnamed x1, blocking collectives  15.2 us
  transfers between devices with their start and end apart: 2, of which 2 were waited for; matrix products, arithmetic and copies ran while one was open for 1% of the time, Pallas kernels for 0%

commit v1 on v0

--- a/solution.py
+++ b/solution.py
@@ -100,7 +100,7 @@
     start = (jnp.zeros((params, params), jnp.float32), jnp.zeros((params,), jnp.float32))
     gram_part, grad_part = lax.fori_loop(0, trips, add_block, start)
     live_part = jnp.sum(pick(live))
-    gram, grad, total = lax.psum((gram_part, grad_part, live_part), ("rows", "cols"))
+    gram, grad, total = lax.psum(lax.psum((gram_part, grad_part, live_part), "rows"), "cols")
     normal = gram / total + damping * jnp.eye(params, dtype=jnp.float32)
     lower = jnp.linalg.cholesky(normal)
     step = solve_step(lower, grad / total)

time: 712 us -> 671 us (0.942)
  the two profiles are of different devices: /device:TPU:8 before, /device:TPU:1 now
where the time goes in v1:
time: 671 us; the launch traced here: 664 us
  waiting for transfers between devices  273 us (41%)
  blocking collectives  176 us (26%)
  other arithmetic  133 us (20%)
  local copies, waits for them, and re-layouts  37.7 us (6%)
  between operations  22.7 us (3%)
  matrix products  10.9 us (2%)
  starting transfers between devices  10.3 us (2%)
    psum x1, waiting for transfers between devices, on_device(): lax.psum((gram_part, grad_part, live_part), 'rows')  264 us
    psum x1, blocking collectives, on_device(): lax.psum((gram_part, grad_part, live_part), 'rows')  112 us
    another operation x14, other arithmetic, on_device(): lower = jnp.linalg.cholesky(normal)  78.7 us
    psum x1, blocking collectives, on_device(): lax.psum(lax.psum((gram_part, grad_part, live_part), 'rows'), 'cols')  51.1 us
    another operation x3, other arithmetic, solve_step(): lax.linalg.triangular_solve(lower, inner, left_side=True, lower=True, tra...  41.4 us
  transfers between devices with their start and end apart: 3, of which 2 were waited for; matrix products, arithmetic and copies ran while one was open for 1% of the time, Pallas kernels for 0%

profile of v1, /device:TPU:1, one launch (start us, length us, event | category | flops | bytes accessed | tf_op | source)
XLA Modules:
  0.0 663.9 jit_solution(13950084827675563554)
XLA Ops:
  16.3 1.0 convolution_bitcast_fusion
  17.3 1.1 fusion.15
  18.4 8.6 %copy.61 = f32[8,8,32,128]{0,3,2,1:T(8,128)} copy(f32[8,8,32,128]{3,2,1,0:T(8,128)S(1)} %fusion.15) | data formatting | bytes 2097152 | tf_op jit(solution)/shard_map/reshape | solution.py:44
  27.0 11.2 %gather_fusion = f32[2048,8]{1,0:T(8,128)S(1)} fusion(f32[8,32768]{0,1:T(8,128)} %bitcast.185, s32[2048]{0:T(1024)S(1)} %fusion.50), kind=kCustom, calls=%fused_computation | custom fusion | bytes 139264 | tf_op jit(solution)/shard_map/jit(_take)/gather | solution.py:70
  38.8 1.3 convolution_tanh_fusion
  40.6 1.0 copy.43
  41.5 10.2 %all-to-all-start = ((f32[8,256,64]{1,2,0:T(8,128)}), f32[8,256,64]{1,2,0:T(8,128)S(1)}, u32[]{:S(2)}, u32[]{:S(2)}) async-start(f32[8,256,64]{1,2,0:T(8,128)} %copy.43), calls=%async_computation | async-start | bytes 1048576 | tf_op jit(solution)/shard_map/all_to_all | solution.py:85
  52.1 0.8 dynamic-slice_select_fusion
  52.9 8.2 %all-to-all-done = f32[8,256,64]{1,2,0:T(8,128)S(1)} async-done(((f32[8,256,64]{1,2,0:T(8,128)}), f32[8,256,64]{1,2,0:T(8,128)S(1)}, u32[]{:S(2)}, u32[]{:S(2)}) %all-to-all-start) | async-done | bytes 524320 | tf_op jit(solution)/shard_map/all_to_all | solution.py:85
  61.1 1.0 fusion.83
  63.2 1.3 copy.45
  64.6 264.4 %all-reduce.7.cloned.1.call-done = f32[512,512]{0,1:T(8,128)} async-done(((f32[512,512]{0,1:T(8,128)}), f32[512,512]{0,1:T(8,128)}) %all-reduce.7.cloned.1.call-update) | async-done | bytes 1048592 | tf_op jit(solution)/shard_map/psum | solution.py:103
  330.4 1.3 dynamic-slice.4
  332.3 112.5 %all-reduce.2 = (f32[]{:T(128)}, f32[512]{0:T(512)S(1)}) all-reduce(f32[]{:T(128)} %dynamic-slice_reduce_fusion, f32[512]{0:T(512)S(1)} %get-tuple-element.82), channel_id=1, replica_groups=mesh['rows'=64,'cols'=8] {'rows'}, use_global_device_ids=true, to_apply=%region_10.0 | all-reduce | flops 513 | bytes 4104 | tf_op jit(solution)/shard_map/psum | solution.py:103
  444.8 51.1 %all-reduce.3 = (f32[]{:T(128)}, f32[512]{0:T(512)S(1)}) all-reduce(f32[]{:T(128)} %get-tuple-element.147, f32[512]{0:T(512)S(1)} %get-tuple-element.148), channel_id=1, replica_groups=mesh['rows'=64,'cols'=8] {'cols'}, use_global_device_ids=true, to_apply=%region_11.0 | all-reduce | flops 513 | bytes 4104 | tf_op jit(solution)/shard_map/psum | solution.py:103
  496.6 2.0 select_add_fusion
  499.0 2.1 fusion.12
  501.1 11.7 %cholesky.103 = f32[128,128]{1,0:T(8,128)S(1)} custom-call(f32[128,128]{1,0:T(8,128)S(1)} %cholesky.263), custom_call_target="Cholesky" | custom-call | tf_op jit(solution)/shard_map/jit(cholesky)/cholesky | solution.py:105
  512.9 9.8 %custom-call.32 = f32[1,128,128]{1,2,0:T(8,128)S(1)} custom-call(f32[1,128,128]{2,1,0:T(8,128)S(1)} %get-tuple-element.164), custom_call_target="InvertDiagBlocksLowerTriangular" | custom-call | tf_op jit(solution)/shard_map/jit(cholesky)/cholesky | solution.py:105
  523.4 11.7 %cholesky.215 = f32[128,128]{1,0:T(8,128)S(1)} custom-call(f32[128,128]{1,0:T(8,128)S(1)} %cholesky.267), custom_call_target="Cholesky" | custom-call | tf_op jit(solution)/shard_map/jit(cholesky)/cholesky | solution.py:105
  535.6 9.9 %custom-call.33 = f32[1,128,128]{1,2,0:T(8,128)S(1)} custom-call(f32[1,128,128]{2,1,0:T(8,128)S(1)} %get-tuple-element.162), custom_call_target="InvertDiagBlocksLowerTriangular" | custom-call | tf_op jit(solution)/shard_map/jit(cholesky)/cholesky | solution.py:105
  546.5 11.7 %cholesky.236 = f32[128,128]{1,0:T(8,128)S(1)} custom-call(f32[128,128]{1,0:T(8,128)S(1)} %cholesky.272), custom_call_target="Cholesky" | custom-call | tf_op jit(solution)/shard_map/jit(cholesky)/cholesky | solution.py:105
  558.4 9.8 %custom-call.34 = f32[1,128,128]{1,2,0:T(8,128)S(1)} custom-call(f32[1,128,128]{2,1,0:T(8,128)S(1)} %get-tuple-element.160), custom_call_target="InvertDiagBlocksLowerTriangular" | custom-call | tf_op jit(solution)/shard_map/jit(cholesky)/cholesky | solution.py:105
  569.0 11.9 %cholesky.253 = f32[128,128]{1,0:T(8,128)S(1)} custom-call(f32[128,128]{1,0:T(8,128)S(1)} %convolution_subtract_fusion.2), custom_call_target="Cholesky" | custom-call | tf_op jit(solution)/shard_map/jit(cholesky)/cholesky | solution.py:105
  585.5 1.2 fusion.13
  586.8 11.3 %while.16 = (s32[]{:T(128)}, f32[512,512]{0,1:T(8,128)S(1)}, s32[4,2]{0,1:T(2,128)S(1)}, f32[4,128,128]{2,1,0:T(8,128)}, s32[]{:T(128)}) while((s32[]{:T(128)}, f32[512,512]{0,1:T(8,128)S(1)}, s32[4,2]{0,1:T(2,128)S(1)}, f32[4,128,128]{2,1,0:T(8,128)}, s32[]{:T(128)}) %tuple.61), condition=%wide.while_cond, body=%wide.while_body.sunk | while | flops 2 | bytes 393829 | solution.py:53
  587.5 1.4 dynamic-slice.12
  590.3 1.4 dynamic-slice.12
  593.1 1.4 dynamic-slice.12
  595.9 1.4 dynamic-slice.12
  598.1 40.1 %custom-call.35 = f32[4,128,128]{1,2,0:T(8,128)S(1)} custom-call(f32[4,128,128]{2,1,0:T(8,128)} %get-tuple-element.90), custom_call_target="InvertDiagBlocksLowerTriangular" | custom-call | tf_op jit(solution)/shard_map/triangular_solve | solution.py:53
  642.8 12.6 %all-reduce.1 = f32[2048]{0:T(1024)S(1)} all-reduce(f32[2048]{0:T(1024)S(1)} %bitcast.197), channel_id=2, replica_groups=mesh['rows'=64,'cols'=8] {'cols'}, use_global_device_ids=true, to_apply=%region_22.23.clone | all-reduce | flops 2048 | bytes 16384
  (120 shorter events, 26.1 us)
Async XLA Ops:
  7.2 9.1 %copy-start = (f32[8,32,128]{2,1,0:T(8,128)S(1)}, f32[8,32,128]{2,1,0:T(8,128)}, u32[]{:S(2)}) copy-start(f32[8,32,128]{2,1,0:T(8,128)} %param.10) | copy-start | bytes 393220
  7.2 31.7 %copy-start.1 = (f32[64,8]{0,1:T(8,128)S(1)}, f32[64,8]{0,1:T(8,128)}, u32[]{:S(2)}) copy-start(f32[64,8]{0,1:T(8,128)} %param.15) | copy-start | bytes 6148
  7.2 33.0 %copy-start.3 = (f32[64]{0:T(128)S(1)}, f32[64]{0:T(128)}, u32[]{:S(2)}) copy-start(f32[64]{0:T(128)} %param.16) | copy-start | bytes 772
  7.2 33.1 %copy-start.2 = (s32[2048]{0:T(1024)S(1)}, s32[2048]{0:T(1024)}, u32[]{:S(2)}) copy-start(s32[2048]{0:T(1024)} %param.12) | copy-start | bytes 24580
  41.5 19.6 %all-to-all-start = ((f32[8,256,64]{1,2,0:T(8,128)}), f32[8,256,64]{1,2,0:T(8,128)S(1)}, u32[]{:S(2)}, u32[]{:S(2)}) async-start(f32[8,256,64]{1,2,0:T(8,128)} %copy.43), calls=%async_computation | async-start | bytes 1048576 | tf_op jit(solution)/shard_map/all_to_all | solution.py:85
  51.8 277.2 %all-reduce.7.cloned.1.call-start = ((), (), s32[]{:S(2)}) async-start(), calls=%async_computation.1 | async-start | bytes 2097152 | tf_op jit(solution)/shard_map/psum | solution.py:103
  64.5 432.1 %all-reduce.9.cloned.1.call-start = ((), (), s32[]{:S(2)}) async-start(), calls=%async_computation.2 | async-start | bytes 2097152 | tf_op jit(solution)/shard_map/psum | solution.py:103
Sparse Core Ops, SparseCore 0:
  64.6 264.2 all-reduce.6
  331.3 81.2 all-reduce.8
